TPU v7x, 256 devices: a whole 4x4x8 slice. The times are simulated.
256 devices in a mesh: space: 32 (over x, z_hi, y), ens: 8 (over z_lo, core).
Axes of the slice: x: 4, y: 4, z: 8 (z_hi: 2, z_lo: 4; z = z_hi * 4 + z_lo), core: 2. Of those that a mesh axis runs over, the one named last changes fastest.
Arguments:
- outlook_array: bfloat16 [1536, 49152], P('ens', 'space'), may hold values from -57 to 57
- earlier_location_basis: bfloat16 [49152, 256], P('space'), may hold values from -4 to 4
- earlier_ensemble_basis: float32 [48, 16], replicated, may hold values from -4 to 4
- earlier_height_basis: float32 [32, 16], replicated, may hold values from -4 to 4
Outputs:
- spatial_factor: float32 [49152, 256], P(('space', 'ens'))
- member_factor: float32 [48, 16], replicated
- level_factor: float32 [32, 16], replicated
All inputs are finite; a program needn't handle non-finite values.
Results may differ from a plain program's by a relative error of at most 0.0075.
The roundings to bfloat16 on the way count: a program that leaves them out, or rounds other values in their place, can miss the bound.
Values may be sent and summed in bfloat16 or wider, within the bound.
A program may use at most 64 MiB of HBM per device.

v0:
```python
import jax
import jax.numpy as jnp
from jax import lax
from jax.sharding import PartitionSpec as P

MEMBERS = 48
LEVELS = 32
PASSES = 3


highest = lax.Precision.HIGHEST


def inner_gram(image_rows):
    return lax.dot_general(
        image_rows,
        image_rows,
        (((0,), (0,)), ((), ())),
        precision=highest,
        preferred_element_type=jnp.float32,
    )


def solve_right(lower_factor, image_rows):
    return lax.linalg.triangular_solve(
        lower_factor, image_rows, left_side=False, lower=True, transpose_a=True
    )


def refine(gram_matrix, previous, row_count):
    image_rows = jnp.dot(
        gram_matrix, previous, precision=highest, preferred_element_type=jnp.float32
    )
    lower_factor = jnp.linalg.cholesky(inner_gram(image_rows) / row_count)
    return solve_right(lower_factor, image_rows)


def factor_grams(final_band_lines):
    by_level = final_band_lines.reshape(LEVELS, -1)
    level_gram = jnp.dot(by_level, by_level.T, preferred_element_type=jnp.float32)
    by_member = (
        final_band_lines.reshape(LEVELS, MEMBERS, -1).transpose(1, 0, 2).reshape(MEMBERS, -1)
    )
    member_gram = jnp.dot(by_member, by_member.T, preferred_element_type=jnp.float32)
    return (member_gram, level_gram)


def spatial_step(ensemble_variance, grid_total):
    gram_total = lax.psum(inner_gram(ensemble_variance), ("space", "ens")) / grid_total
    return solve_right(jnp.linalg.cholesky(gram_total), ensemble_variance)


def project(vertical_cells, location_basis_matrix):
    row_share = lax.psum_scatter(
        jnp.dot(vertical_cells, location_basis_matrix, preferred_element_type=jnp.float32),
        "ens",
        scatter_dimension=0,
        tiled=True,
    )
    row_share = lax.psum(row_share, "space")
    return lax.all_gather(row_share.astype(jnp.bfloat16), "ens", axis=0, tiled=True)


def on_device(outlook_array, earlier_location_basis, earlier_ensemble_basis, earlier_height_basis):
    ens_count = lax.axis_size("ens")
    grid_dev = earlier_location_basis.shape[0]
    sub_rows = grid_dev // ens_count
    grid_total = grid_dev * lax.axis_size("space")
    factor = None
    final_band_lines = None
    vertical_cells = lax.all_to_all(outlook_array, "ens", split_axis=1, concat_axis=0, tiled=True)
    first_row = lax.axis_index("ens") * sub_rows
    location_basis_matrix = lax.dynamic_slice_in_dim(earlier_location_basis, first_row, sub_rows, 0)
    for pass_index in range(PASSES + 1):
        final_band_lines = project(vertical_cells, location_basis_matrix)
        if pass_index < PASSES:
            ensemble_variance = lax.dot_general(
                vertical_cells,
                final_band_lines,
                (((0,), (0,)), ((), ())),
                preferred_element_type=jnp.float32,
            )
            factor = spatial_step(ensemble_variance, grid_total)
            location_basis_matrix = factor.astype(jnp.bfloat16)
    member_gram, level_gram = factor_grams(final_band_lines)
    return (
        factor,
        refine(member_gram, earlier_ensemble_basis, MEMBERS),
        refine(level_gram, earlier_height_basis, LEVELS),
    )


def solution(mesh):
    in_specs = (P("ens", "space"), P("space", None), P(), P())
    out_specs = (P(("space", "ens"), None), P(), P())
    return jax.shard_map(
        on_device, mesh=mesh, in_specs=in_specs, out_specs=out_specs, check_vma=False
    )
```

profile of v0, /device:TPU:1, one launch (start us, length us, event | category | flops | bytes accessed | tf_op | source)
XLA Modules:
  0.0 2115.9 jit_solution(5704616628953250704)
XLA Ops:
  9.5 7.4 all-to-all-start
  16.9 20.0 all-to-all-done
  40.1 37.7 %reduce-scatter.13.cloned.1.call-done = f32[192,256]{1,0:T(8,128)} async-done(((f32[1536,256]{1,0:T(8,128)}), f32[192,256]{1,0:T(8,128)}) %reduce-scatter.13.cloned.1.call-update) | async-done | bytes 196624 | tf_op jit(solution)/shard_map/reduce_scatter | solution.py:54
  77.8 198.7 %all-reduce.14 = bf16[192,256]{1,0:T(8,128)(2,1)S(1)} all-reduce(f32[192,256]{1,0:T(8,128)} %reduce-scatter.13.cloned.1.call-done), channel_id=1, replica_groups=mesh['space'=32,'ens'=8] {'space'}, use_global_device_ids=true, to_apply=%region_1.0 | all-reduce | flops 49152 | bytes 294912 | tf_op jit(solution)/shard_map/psum | solution.py:60
  276.4 44.7 %all_gather.12 = bf16[1536,256]{1,0:T(8,128)(2,1)S(1)} all-gather(bf16[192,256]{1,0:T(8,128)(2,1)S(1)} %all-reduce.14), channel_id=1, replica_groups=mesh['space'=32,'ens'=8] {'ens'}, dimensions={0}, use_global_device_ids=true | all-gather | bytes 884736 | tf_op jit(solution)/shard_map/all_gather | solution.py:61
  323.4 243.8 %all-reduce.9.cloned.1.call-done = f32[256,256]{0,1:T(8,128)} async-done(((f32[256,256]{0,1:T(8,128)}), f32[256,256]{0,1:T(8,128)}) %all-reduce.9.cloned.1.call-update) | async-done | bytes 262160 | tf_op jit(solution)/shard_map/psum | solution.py:49
  569.3 11.7 cholesky.214
  581.1 9.8 custom-call.25
  591.4 11.7 cholesky.231
  605.3 4.3 while.6
  609.6 19.7 custom-call.26
  632.2 37.2 %reduce-scatter.15.cloned.1.call-done = f32[192,256]{1,0:T(8,128)} async-done(((f32[1536,256]{1,0:T(8,128)}), f32[192,256]{1,0:T(8,128)}) %reduce-scatter.15.cloned.1.call-update) | async-done | bytes 196624 | tf_op jit(solution)/shard_map/reduce_scatter | solution.py:54
  669.3 198.6 %all-reduce.15 = bf16[192,256]{1,0:T(8,128)(2,1)S(1)} all-reduce(f32[192,256]{1,0:T(8,128)} %reduce-scatter.15.cloned.1.call-done), channel_id=1, replica_groups=mesh['space'=32,'ens'=8] {'space'}, use_global_device_ids=true, to_apply=%region_8.11 | all-reduce | flops 49152 | bytes 294912 | tf_op jit(solution)/shard_map/psum | solution.py:60
  867.9 44.7 %all_gather.13 = bf16[1536,256]{1,0:T(8,128)(2,1)S(1)} all-gather(bf16[192,256]{1,0:T(8,128)(2,1)S(1)} %all-reduce.15), channel_id=1, replica_groups=mesh['space'=32,'ens'=8] {'ens'}, dimensions={0}, use_global_device_ids=true | all-gather | bytes 884736 | tf_op jit(solution)/shard_map/all_gather | solution.py:61
  914.4 244.5 %all-reduce.11.cloned.1.call-done = f32[256,256]{0,1:T(8,128)} async-done(((f32[256,256]{0,1:T(8,128)}), f32[256,256]{0,1:T(8,128)}) %all-reduce.11.cloned.1.call-update) | async-done | bytes 262160 | tf_op jit(solution)/shard_map/psum | solution.py:49
  1161.1 11.7 cholesky.248
  1172.8 9.8 custom-call.27
  1183.1 11.7 cholesky.265
  1197.6 4.5 while.7
  1202.1 19.7 custom-call.28
  1224.7 37.2 %reduce-scatter.17.cloned.1.call-done = f32[192,256]{1,0:T(8,128)} async-done(((f32[1536,256]{1,0:T(8,128)}), f32[192,256]{1,0:T(8,128)}) %reduce-scatter.17.cloned.1.call-update) | async-done | bytes 196624 | tf_op jit(solution)/shard_map/reduce_scatter | solution.py:54
  1261.9 198.8 %all-reduce.16 = bf16[192,256]{1,0:T(8,128)(2,1)S(1)} all-reduce(f32[192,256]{1,0:T(8,128)} %reduce-scatter.17.cloned.1.call-done), channel_id=1, replica_groups=mesh['space'=32,'ens'=8] {'space'}, use_global_device_ids=true, to_apply=%region_11.14 | all-reduce | flops 49152 | bytes 294912 | tf_op jit(solution)/shard_map/psum | solution.py:60
  1460.7 44.6 %all_gather.14 = bf16[1536,256]{1,0:T(8,128)(2,1)S(1)} all-gather(bf16[192,256]{1,0:T(8,128)(2,1)S(1)} %all-reduce.16), channel_id=1, replica_groups=mesh['space'=32,'ens'=8] {'ens'}, dimensions={0}, use_global_device_ids=true | all-gather | bytes 884736 | tf_op jit(solution)/shard_map/all_gather | solution.py:61
  1507.1 244.3 %all-reduce.13.cloned.1.call-done = f32[256,256]{0,1:T(8,128)} async-done(((f32[256,256]{0,1:T(8,128)}), f32[256,256]{0,1:T(8,128)}) %all-reduce.13.cloned.1.call-update) | async-done | bytes 262160 | tf_op jit(solution)/shard_map/psum | solution.py:49
  1753.5 11.7 cholesky.282
  1765.3 9.8 custom-call.29
  1775.6 11.7 cholesky.299
  1790.0 4.2 while.8
  1794.2 19.7 custom-call.30
  1816.7 37.2 %reduce-scatter.19.cloned.1.call-done = f32[192,256]{1,0:T(8,128)} async-done(((f32[1536,256]{1,0:T(8,128)}), f32[192,256]{1,0:T(8,128)}) %reduce-scatter.19.cloned.1.call-update) | async-done | bytes 196624 | tf_op jit(solution)/shard_map/reduce_scatter | solution.py:54
  1853.9 198.8 %all-reduce.17 = bf16[192,256]{1,0:T(8,128)(2,1)S(1)} all-reduce(f32[192,256]{1,0:T(8,128)} %reduce-scatter.19.cloned.1.call-done), channel_id=1, replica_groups=mesh['space'=32,'ens'=8] {'space'}, use_global_device_ids=true, to_apply=%region_14.17 | all-reduce | flops 49152 | bytes 294912 | tf_op jit(solution)/shard_map/psum | solution.py:60
  2052.7 44.6 %all_gather.15 = bf16[1536,256]{1,0:T(8,128)(2,1)S(1)} all-gather(bf16[192,256]{1,0:T(8,128)(2,1)S(1)} %all-reduce.17), channel_id=1, replica_groups=mesh['space'=32,'ens'=8] {'ens'}, dimensions={0}, use_global_device_ids=true | all-gather | bytes 884736 | tf_op jit(solution)/shard_map/all_gather | solution.py:61
  (130 shorter events, 54.7 us)
Async XLA Ops:
  7.2 30.8 %copy-start = (bf16[1536,256]{1,0:T(8,128)(2,1)S(1)}, bf16[1536,256]{1,0:T(8,128)(2,1)}, u32[]{:S(2)}) copy-start(bf16[1536,256]{1,0:T(8,128)(2,1)} %param.9) | copy-start | bytes 2359300
  9.5 27.4 %all-to-all-start = ((bf16[192,8,192]{0,2,1:T(8,128)(2,1)}), bf16[192,8,192]{0,2,1:T(8,128)(2,1)S(1)}, u32[]{:S(2)}, u32[]{:S(2)}) async-start(bf16[192,8,192]{0,2,1:T(8,128)(2,1)} %bitcast), calls=%async_computation | async-start | bytes 1572864 | tf_op jit(solution)/shard_map/all_to_all | solution.py:71
  16.9 60.9 %reduce-scatter.13.cloned.1.call-start = ((), (), s32[]{:S(2)}) async-start(), calls=%async_computation.8 | async-start | bytes 1769472 | tf_op jit(solution)/shard_map/reduce_scatter | solution.py:54
  40.0 527.2 %all-reduce.9.cloned.1.call-start = ((), (), s32[]{:S(2)}) async-start(), calls=%async_computation.5 | async-start | bytes 524288 | tf_op jit(solution)/shard_map/psum | solution.py:49
  322.8 346.5 %reduce-scatter.15.cloned.1.call-start = ((), (), s32[]{:S(2)}) async-start(), calls=%async_computation.9 | async-start | bytes 1769472 | tf_op jit(solution)/shard_map/reduce_scatter | solution.py:54
  632.1 526.8 %all-reduce.11.cloned.1.call-start = ((), (), s32[]{:S(2)}) async-start(), calls=%async_computation.6 | async-start | bytes 524288 | tf_op jit(solution)/shard_map/psum | solution.py:49
  914.3 347.6 %reduce-scatter.17.cloned.1.call-start = ((), (), s32[]{:S(2)}) async-start(), calls=%async_computation.10 | async-start | bytes 1769472 | tf_op jit(solution)/shard_map/reduce_scatter | solution.py:54
  1224.6 526.8 %all-reduce.13.cloned.1.call-start = ((), (), s32[]{:S(2)}) async-start(), calls=%async_computation.7 | async-start | bytes 524288 | tf_op jit(solution)/shard_map/psum | solution.py:49
  1507.1 346.9 %reduce-scatter.19.cloned.1.call-start = ((), (), s32[]{:S(2)}) async-start(), calls=%async_computation.11 | async-start | bytes 1769472 | tf_op jit(solution)/shard_map/reduce_scatter | solution.py:54
  1814.6 2.0 copy-start.1
  2097.3 0.7 copy-start.3
  2097.7 5.9 copy-start.2
Sparse Core Ops, SparseCore 0:
  40.1 37.5 reduce-scatter.12
  323.0 244.1 all-reduce.8
  632.2 37.0 reduce-scatter.14
  914.5 244.4 all-reduce.10
  1224.8 37.0 reduce-scatter.16
  1507.2 244.1 all-reduce.12
  1816.8 37.0 reduce-scatter.18
where the time goes:
time: 2120 us
  blocking collectives  973 us (46%)
  waiting for transfers between devices  902 us (43%)
  other arithmetic  176 us (8%)
  local copies, waits for them, and re-layouts  23.1 us (1%)
    psum x4, blocking collectives, project(): row_share = lax.psum(row_share, 'space')  795 us
    psum x3, waiting for transfers between devices, spatial_step(): lax.psum(inner_gram(ensemble_variance), ('space', 'ens')) / grid_total  733 us
    all_gather x4, blocking collectives, project(): lax.all_gather(row_share.astype(jnp.bfloat16), 'ens', axis=0, tiled=True)  179 us
    reduce_scatter x4, waiting for transfers between devices, project(): lax.psum_scatter(jnp.dot(vertical_cells, location_basis_matrix, preferred...  149 us
    another operation x20, other arithmetic, spatial_step(): return solve_right(jnp.linalg.cholesky(gram_total), ensemble_variance)  103 us
    another operation x12, other arithmetic, solve_right(): lax.linalg.triangular_solve(lower_factor, image_rows, left_side=False, lo...  62.9 us
  transfers between devices with their start and end apart: 8, of which 8 were waited for; matrix products, arithmetic and copies ran while one was open for 0% of the time, Pallas kernels for 0%

commit v1 on v0

v1 whole, which is shorter than its diff:
```python
import functools

import jax
import jax.numpy as jnp
from jax import lax
from jax.experimental import pallas as pl
from jax.experimental.pallas import tpu as pltpu
from jax.sharding import PartitionSpec as P

MEMBERS = 48
LEVELS = 32
PASSES = 3
RANK = 256
ROWS = 1536
GRID = 49152
EXACT = lax.Precision.HIGHEST

BLOCK = 256
BLOCKS = 7
PACKED = 28 * 2 * BLOCK
HALF = PACKED // 2
RING1 = HALF // 4
RING2 = RING1 // 4
LEAF = RING2 // 8
CHIP_COLS = 384
SHARD_ROWS = 192


def nt(a, b, precision=None):
    return lax.dot_general(
        a, b, (((1,), (1,)), ((), ())), precision=precision, preferred_element_type=jnp.float32
    )


def tn(a, b, precision=None):
    return lax.dot_general(
        a, b, (((0,), (0,)), ((), ())), precision=precision, preferred_element_type=jnp.float32
    )


def nn(a, b, precision=None):
    return jnp.dot(a, b, precision=precision, preferred_element_type=jnp.float32)


def exchange_kernel(
    x_ref, b_ref, out, xg, acc, aug, r1h, r1f, a2, r2h, r2f, a3, zbuf, send, recv
):
    s = lax.axis_index("space")
    e = lax.axis_index("ens")
    x, zh, y = s // 8, (s // 4) % 2, s % 4
    zl, c = e // 2, e % 2
    z = zh * 4 + zl
    st1, st2 = 8 - 7 * c, 1 + 7 * c
    p1 = x * (1 - c) + y * c
    p2 = y * (1 - c) + x * c

    def device(space, ens):
        return {"space": space, "ens": ens}

    partner = device(s, zl * 2 + 1 - c)

    def ring(p, st):
        right, left = (p + 1) % 4, (p + 3) % 4
        return (
            device(s + (right - p) * st, e),
            device(s + (left - p) * st, e),
            right,
            left,
            (p + 2) % 4,
        )

    ring1, ring2 = ring(p1, st1), ring(p2, st2)
    zpeers = []
    for k in range(1, 8):
        other = (z + k) % 8
        zpeers.append((device(x * 8 + (other // 4) * 4 + y, (other % 4) * 2 + c), other))

    barrier = pltpu.get_barrier_semaphore()
    greeted = [partner, ring1[0], ring1[1], ring2[0], ring2[1]] + [d for d, _ in zpeers]
    for d in greeted:
        pl.semaphore_signal(barrier, inc=1, device_id=d, device_id_type=pl.DeviceIdType.MESH)
    pl.semaphore_wait(barrier, len(greeted))

    used = [0]
    pending = []

    def start(src, dst, dev):
        n = used[0]
        used[0] += 1
        copy = pltpu.make_async_remote_copy(
            src_ref=src,
            dst_ref=dst,
            send_sem=send.at[n],
            recv_sem=recv.at[n],
            device_id=dev,
            device_id_type=pl.DeviceIdType.MESH,
        )
        copy.start()
        pending.append(copy)
        return copy

    def rows(first, count):
        return pl.ds(pl.multiple_of(first, 8), count)

    def slab_rows(chip, core):
        return pl.ds(pl.multiple_of((chip * 2 + core) * SHARD_ROWS, 64), SHARD_ROWS)

    def chip_cols(chip):
        return pl.ds(pl.multiple_of(chip * CHIP_COLS, 128), CHIP_COLS)

    mine = slab_rows(zl, c)
    moved = []
    for k in range(1, 4):
        to = (zl + k) % 4
        moved.append(start(x_ref.at[:, chip_cols(to)], xg.at[mine, :], device(s, to * 2 + c)))
    xg[mine, :] = x_ref[:, chip_cols(zl)]
    shared = [start(xg.at[mine, :], xg.at[mine, :], partner)]
    part = b_ref[pl.ds(pl.multiple_of(zl * CHIP_COLS, 128), CHIP_COLS), :]
    aug[pl.ds(ROWS, BLOCK), :] = part.astype(jnp.float32).T.astype(jnp.bfloat16)
    for k in range(1, 4):
        moved[k - 1].wait_recv()
        got = slab_rows((zl + 4 - k) % 4, c)
        shared.append(start(xg.at[got, :], xg.at[got, :], partner))
    for copy in shared:
        copy.wait_recv()
    aug[pl.ds(0, ROWS), :] = xg[...]

    @pl.loop(0, 14)
    def _(k):
        t = c * 14 + k
        i = t % BLOCKS
        j = (i + t // BLOCKS) % BLOCKS
        a = aug[pl.ds(pl.multiple_of(i * BLOCK, BLOCK), BLOCK), :]
        b = aug[pl.ds(pl.multiple_of(j * BLOCK, BLOCK), BLOCK), :]
        product = nt(a, b)
        acc[pl.ds(pl.multiple_of(k * 512, 512), 256), :] = product[:, :128]
        acc[pl.ds(pl.multiple_of(k * 512 + 256, 256), 256), :] = product[:, 128:]

    def reduce_ring(a, half_in, full_in, place, p, piece, result):
        to_right, to_left, right, left, opp = place
        h = piece // 2
        c1 = start(a.at[rows(opp * piece, h), :], half_in.at[0], to_right)
        c3 = start(a.at[rows(opp * piece + h, h), :], half_in.at[1], to_left)
        c2 = start(a.at[rows(right * piece + h, h), :], full_in.at[0, pl.ds(h, h), :], to_right)
        c4 = start(a.at[rows(left * piece, h), :], full_in.at[1, pl.ds(0, h), :], to_left)
        c1.wait_recv()
        a[rows(right * piece, h), :] = a[rows(right * piece, h), :] + half_in[0]
        c5 = start(a.at[rows(right * piece, h), :], full_in.at[0, pl.ds(0, h), :], to_right)
        c3.wait_recv()
        a[rows(left * piece + h, h), :] = a[rows(left * piece + h, h), :] + half_in[1]
        c6 = start(a.at[rows(left * piece + h, h), :], full_in.at[1, pl.ds(h, h), :], to_left)
        for copy in (c2, c4, c5, c6):
            copy.wait_recv()
        result[...] = a[rows(p * piece, piece), :] + full_in[0] + full_in[1]

    reduce_ring(acc, r1h, r1f, ring1, p1, RING1, a2)
    reduce_ring(a2, r2h, r2f, ring2, p2, RING2, a3)
    copies = [
        start(a3.at[rows(other * LEAF, LEAF), :], zbuf.at[k], d)
        for k, (d, other) in enumerate(zpeers)
    ]
    total = a3[rows(z * LEAF, LEAF), :]
    for k, copy in enumerate(copies):
        copy.wait_recv()
        total = total + zbuf[k]

    base1 = c * HALF
    base2 = base1 + p1 * RING1
    base3 = base2 + p2 * RING2
    leaf = rows(base3 + z * LEAF, LEAF)
    out[leaf, :] = total
    copies = [start(out.at[leaf, :], out.at[leaf, :], d) for d, _ in zpeers]
    for copy in copies:
        copy.wait_recv()

    def gather_ring(base, place, p, piece, on_piece):
        to_right, to_left, right, left, _ = place
        h = piece // 2

        def part(q, half):
            return rows(base + q * piece + half * h, h)

        def put(q, half, dev):
            return start(out.at[part(q, half), :], out.at[part(q, half), :], dev)

        r1 = put(p, 0, to_right)
        l1 = put(p, 1, to_left)
        r2 = put(p, 1, to_right)
        l2 = put(p, 0, to_left)
        on_piece(rows(base + p * piece, piece))
        r1.wait_recv()
        r3 = put(left, 0, to_right)
        on_piece(part(left, 0))
        l1.wait_recv()
        l3 = put(right, 1, to_left)
        on_piece(part(right, 1))
        r2.wait_recv()
        on_piece(part(left, 1))
        l2.wait_recv()
        on_piece(part(right, 0))
        r3.wait_recv()
        opp = (p + 2) % 4
        on_piece(part(opp, 0))
        l3.wait_recv()
        on_piece(part(opp, 1))

    gather_ring(base2, ring2, p2, RING2, lambda where: None)
    across = []
    gather_ring(
        base1,
        ring1,
        p1,
        RING1,
        lambda where: across.append(start(out.at[where, :], out.at[where, :], partner)),
    )
    for copy in across:
        copy.wait_recv()
    for copy in pending:
        copy.wait_send()


def exchange(outlook, basis):
    f32, bf16 = jnp.float32, jnp.bfloat16
    vmem = pl.BlockSpec(memory_space=pltpu.VMEM)
    copies = 64
    return pl.pallas_call(
        exchange_kernel,
        out_shape=(
            jax.ShapeDtypeStruct((PACKED, 128), f32),
            jax.ShapeDtypeStruct((ROWS, CHIP_COLS), bf16),
        ),
        in_specs=[vmem, vmem],
        out_specs=(vmem, vmem),
        scratch_shapes=[
            pltpu.VMEM((HALF, 128), f32),
            pltpu.VMEM((BLOCKS * BLOCK, CHIP_COLS), bf16),
            pltpu.VMEM((2, RING1 // 2, 128), f32),
            pltpu.VMEM((2, RING1, 128), f32),
            pltpu.VMEM((RING1, 128), f32),
            pltpu.VMEM((2, RING2 // 2, 128), f32),
            pltpu.VMEM((2, RING2, 128), f32),
            pltpu.VMEM((RING2, 128), f32),
            pltpu.VMEM((7, LEAF, 128), f32),
            pltpu.SemaphoreType.DMA((copies,)),
            pltpu.SemaphoreType.DMA((copies,)),
        ],
        compiler_params=pltpu.CompilerParams(
            collective_id=0, has_side_effects=True, vmem_limit_bytes=60 << 20
        ),
        name="moments",
    )(outlook, basis)


def factor_inverse(a, n):
    lanes = 2 * n
    row_id = lax.broadcasted_iota(jnp.int32, (8, lanes), 0)
    unit = (
        lax.broadcasted_iota(jnp.int32, (n, n), 0) == lax.broadcasted_iota(jnp.int32, (n, n), 1)
    ).astype(jnp.float32)
    both = jnp.concatenate([a, unit], axis=1)
    strips = [both[8 * g : 8 * g + 8, :] for g in range(n // 8)]
    scales = [jnp.zeros((8, lanes), jnp.float32) for _ in strips]
    for k in range(n):
        g0, r = divmod(k, 8)
        row = strips[g0][r : r + 1, :]
        pivot = row[:, k : k + 1]
        scales[g0] = jnp.where(row_id == r, lax.rsqrt(pivot), scales[g0])
        step = row * (1.0 / pivot)
        for g in range(g0, n // 8):
            column = strips[g][:, k : k + 1]
            if g == g0:
                column = jnp.where(row_id[:, :1] > r, column, 0.0)
            strips[g] = strips[g] - column * step
    out = jnp.concatenate([v * w for v, w in zip(strips, scales)], axis=0)
    return out[:, n:]


def factor_kernel(packed, xg, factor_ref, final_ref, khi, klo, basis, q, work, spread):
    core = lax.axis_index("ens") % 2
    for t in range(28):
        i = t % BLOCKS
        j = (i + t // BLOCKS) % BLOCKS
        if i == j == BLOCKS - 1:
            continue
        block = jnp.concatenate(
            [packed[pl.ds(t * 512, 256), :], packed[pl.ds(t * 512 + 256, 256), :]], axis=1
        )
        if i == BLOCKS - 1:
            basis[pl.ds(j * BLOCK, BLOCK), :] = block.T.astype(jnp.bfloat16)
            continue
        hi = block.astype(jnp.bfloat16)
        if j == BLOCKS - 1:
            basis[pl.ds(i * BLOCK, BLOCK), :] = hi
            continue
        lo = (block - hi.astype(jnp.float32)).astype(jnp.bfloat16)
        at_i, at_j = pl.ds(i * BLOCK, BLOCK), pl.ds(j * BLOCK, BLOCK)
        khi[at_i, at_j] = hi
        klo[at_i, at_j] = lo
        if i != j:
            khi[at_j, at_i] = hi.astype(jnp.float32).T.astype(jnp.bfloat16)
            klo[at_j, at_i] = lo.astype(jnp.float32).T.astype(jnp.bfloat16)

    unit = (
        lax.broadcasted_iota(jnp.int32, (RANK, RANK), 0)
        == lax.broadcasted_iota(jnp.int32, (RANK, RANK), 1)
    ).astype(jnp.float32)

    def one_pass(index, carry):
        work[:, pl.ds(0, RANK)] = jnp.zeros((RANK, RANK), jnp.float32)
        work[:, pl.ds(RANK, RANK)] = unit

        @pl.loop(0, 6)
        def _(i):
            at = pl.ds(pl.multiple_of(i * BLOCK, BLOCK), BLOCK)
            image = nn(khi[at, :], basis[...]) + nn(klo[at, :], basis[...])
            q[at, :] = image
            work[:, pl.ds(0, RANK)] += tn(basis[at, :].astype(jnp.float32), image, EXACT)

        work[:, pl.ds(0, RANK)] = work[:, pl.ds(0, RANK)] * (1.0 / GRID)
        for p in range(4):
            top = 64 * p
            inverse = factor_inverse(work[pl.ds(top, 64), pl.ds(top, 64)], 64)
            panel = nn(inverse, work[pl.ds(top, 64), :], EXACT)
            work[pl.ds(top, 64), :] = panel
            if p < 3:
                rest = 256 - top - 64
                work[pl.ds(top + 64, rest), :] -= tn(panel[:, top + 64 : 256], panel, EXACT)
        solve = work[:, pl.ds(RANK, RANK)]

        @pl.when(index == PASSES - 1)
        def _():
            spread[...] = tn(xg[...], basis[...])
            own = spread[pl.ds(pl.multiple_of(core * SHARD_ROWS, 64), SHARD_ROWS), :]
            factor_ref[...] = nt(own, solve, EXACT)

        @pl.loop(0, 6)
        def _(i):
            at = pl.ds(pl.multiple_of(i * BLOCK, BLOCK), BLOCK)
            basis[at, :] = nt(q[at, :], solve, EXACT).astype(jnp.bfloat16)

        return carry

    lax.fori_loop(0, PASSES, one_pass, 0)
    final_ref[...] = basis[...]


def factors(packed, xg):
    f32, bf16 = jnp.float32, jnp.bfloat16
    vmem = pl.BlockSpec(memory_space=pltpu.VMEM)
    return pl.pallas_call(
        factor_kernel,
        out_shape=(
            jax.ShapeDtypeStruct((SHARD_ROWS, RANK), f32),
            jax.ShapeDtypeStruct((ROWS, RANK), bf16),
        ),
        in_specs=[vmem, vmem],
        out_specs=(vmem, vmem),
        scratch_shapes=[
            pltpu.VMEM((ROWS, ROWS), bf16),
            pltpu.VMEM((ROWS, ROWS), bf16),
            pltpu.VMEM((ROWS, RANK), bf16),
            pltpu.VMEM((ROWS, RANK), f32),
            pltpu.VMEM((RANK, 2 * RANK), f32),
            pltpu.VMEM((CHIP_COLS, RANK), f32),
        ],
        compiler_params=pltpu.CompilerParams(vmem_limit_bytes=60 << 20),
        name="passes",
    )(packed, xg)


def inner_gram(image_rows):
    return tn(image_rows, image_rows, EXACT)


def solve_right(lower_factor, image_rows):
    return lax.linalg.triangular_solve(
        lower_factor, image_rows, left_side=False, lower=True, transpose_a=True
    )


def refine(gram_matrix, previous, row_count):
    image_rows = nn(gram_matrix, previous, EXACT)
    lower_factor = jnp.linalg.cholesky(inner_gram(image_rows) / row_count)
    return solve_right(lower_factor, image_rows)


def factor_grams(final_band_lines):
    by_level = final_band_lines.reshape(LEVELS, -1)
    level_gram = jnp.dot(by_level, by_level.T, preferred_element_type=jnp.float32)
    by_member = (
        final_band_lines.reshape(LEVELS, MEMBERS, -1).transpose(1, 0, 2).reshape(MEMBERS, -1)
    )
    member_gram = jnp.dot(by_member, by_member.T, preferred_element_type=jnp.float32)
    return (member_gram, level_gram)


def on_device(outlook_array, earlier_location_basis, earlier_ensemble_basis, earlier_height_basis):
    packed, slab = exchange(outlook_array, earlier_location_basis)
    factor, final = factors(packed, slab)
    member_gram, level_gram = factor_grams(final)
    return (
        factor,
        refine(member_gram, earlier_ensemble_basis, MEMBERS),
        refine(level_gram, earlier_height_basis, LEVELS),
    )


def solution(mesh):
    in_specs = (P("ens", "space"), P("space", None), P(), P())
    out_specs = (P(("space", "ens"), None), P(), P())
    return jax.shard_map(
        on_device, mesh=mesh, in_specs=in_specs, out_specs=out_specs, check_vma=False
    )
```

time: 2120 us -> 229 us (0.11)
  blocking collectives: 973 us -> 0 us
  waiting for transfers between devices: 902 us -> 0 us
  Pallas kernels: 0 us -> 214 us
  other arithmetic: 176 us -> 8.05 us
  local copies, waits for them, and re-layouts: 23.1 us -> 1.65 us
    psum x4 -> x0, blocking collectives: 795 us -> none  [project(): row_share = lax.psum(row_share, 'space')]
    psum x3 -> x0, waiting for transfers between devices: 733 us -> none  [spatial_step(): lax.psum(inner_gram(ensemble_variance), ('space', 'ens')) / grid_total]
    pallas_call x0 -> x2, Pallas kernels: none -> 214 us  [the longest x1 110 us: factors(): pl.pallas_call(factor_kernel, out_shape=(jax.ShapeDtypeStruct((SHARD_ROWS...]
    all_gather x4 -> x0, blocking collectives: 179 us -> none  [project(): lax.all_gather(row_share.astype(jnp.bfloat16), 'ens', axis=0, tiled=True)]
    reduce_scatter x4 -> x0, waiting for transfers between devices: 149 us -> none  [project(): lax.psum_scatter(jnp.dot(vertical_cells, location_basis_matrix, preferred...]
    another operation x20 -> x0, other arithmetic: 103 us -> none  [spatial_step(): return solve_right(jnp.linalg.cholesky(gram_total), ensemble_variance)]
    another operation x12 -> x4, other arithmetic: 62.9 us -> 3.75 us  [solve_right(): lax.linalg.triangular_solve(lower_factor, image_rows, left_side=False, lo...]
  transfers between devices with their start and end apart: 8 -> 0, of which waited for: 8 -> 0; matrix products, arithmetic and copies ran while one was open for 0% -> 0% of each run, Pallas kernels for 0% -> 0%
where the time goes in v1:
time: 229 us
  Pallas kernels  214 us (93%)
  other arithmetic  8.05 us (4%)
  matrix products  4.25 us (2%)
    pallas_call x1, Pallas kernels, factors(): pl.pallas_call(factor_kernel, out_shape=(jax.ShapeDtypeStruct((SHARD_ROWS...  110 us
    pallas_call x1, Pallas kernels, exchange(): pl.pallas_call(exchange_kernel, out_shape=(jax.ShapeDtypeStruct((PACKED,...  105 us

profile of v1, /device:TPU:1, one launch (start us, length us, event | category | flops | bytes accessed | tf_op | source)
XLA Modules:
  0.0 229.0 jit_solution(15671314428713778350)
XLA Ops:
  0.6 0.0 copy-start
  0.6 0.0 copy-start.1
  0.7 104.5 %moments.1 = (f32[14336,128]{1,0:T(8,128)}, bf16[1536,384]{1,0:T(8,128)(2,1)}) custom-call(bf16[192,1536]{1,0:T(8,128)(2,1)} %x_ref.1, bf16[1536,256]{1,0:T(8,128)(2,1)} %b_ref.1), custom_call_target="tpu_custom_call" | custom-call | tf_op jit(solution)/shard_map/moments/pallas_call | solution.py:226
  105.2 109.8 %passes.1 = (f32[192,256]{1,0:T(8,128)}, bf16[1536,256]{1,0:T(8,128)(2,1)}) custom-call(f32[14336,128]{1,0:T(8,128)} %get-tuple-element.8.packed, bf16[1536,384]{1,0:T(8,128)(2,1)} %get-tuple-element.9.xg), custom_call_target="tpu_custom_call" | custom-call | tf_op jit(solution)/shard_map/passes/pallas_call | solution.py:350
  215.0 1.7 convolution_bitcast_fusion
  216.7 0.0 copy-done
  216.8 0.1 fusion.8
  216.9 0.2 convolution_multiply_fusion.1
  217.0 0.1 copy.8
  217.1 1.5 cholesky.44
  218.6 0.6 compare_reduce_fusion.1
  219.3 0.6 fusion
  219.9 1.2 custom-call.8
  221.2 0.8 fusion.5
  222.0 1.5 reshape.25
  223.5 0.3 fusion.9
  223.8 0.0 copy-done.1
  223.8 0.1 fusion.10
  223.9 0.1 convolution_multiply_fusion
  224.1 0.1 copy.10
  224.2 1.5 cholesky.55
  225.7 0.6 compare_reduce_fusion
  226.3 0.6 fusion.1
  227.0 1.2 custom-call.9
  228.2 0.8 fusion.2
  (4 shorter events, 0.1 us)
Async XLA Ops:
  0.6 216.1 %copy-start = (f32[48,16]{0,1:T(8,128)S(1)}, f32[48,16]{0,1:T(8,128)}, u32[]{:S(2)}) copy-start(f32[48,16]{0,1:T(8,128)} %param.7) | copy-start | bytes 9220
  0.6 223.1 %copy-start.1 = (f32[32,16]{0,1:T(8,128)S(1)}, f32[32,16]{0,1:T(8,128)}, u32[]{:S(2)}) copy-start(f32[32,16]{0,1:T(8,128)} %param.8) | copy-start | bytes 6148

commit v2 on v1

--- a/solution.py
+++ b/solution.py
@@ -251,28 +251,62 @@
     )(outlook, basis)
 
 
+def split(a):
+    first = a.astype(jnp.bfloat16)
+    rest = a - first.astype(jnp.float32)
+    second = rest.astype(jnp.bfloat16)
+    return first, second, (rest - second.astype(jnp.float32)).astype(jnp.bfloat16)
+
+
 def factor_inverse(a, n):
     lanes = 2 * n
-    row_id = lax.broadcasted_iota(jnp.int32, (8, lanes), 0)
+    full = (8, lanes)
+    row_id = lax.broadcasted_iota(jnp.int32, full, 0)
     unit = (
         lax.broadcasted_iota(jnp.int32, (n, n), 0) == lax.broadcasted_iota(jnp.int32, (n, n), 1)
     ).astype(jnp.float32)
     both = jnp.concatenate([a, unit], axis=1)
-    strips = [both[8 * g : 8 * g + 8, :] for g in range(n // 8)]
-    scales = [jnp.zeros((8, lanes), jnp.float32) for _ in strips]
-    for k in range(n):
-        g0, r = divmod(k, 8)
-        row = strips[g0][r : r + 1, :]
-        pivot = row[:, k : k + 1]
-        scales[g0] = jnp.where(row_id == r, lax.rsqrt(pivot), scales[g0])
-        step = row * (1.0 / pivot)
-        for g in range(g0, n // 8):
-            column = strips[g][:, k : k + 1]
-            if g == g0:
-                column = jnp.where(row_id[:, :1] > r, column, 0.0)
-            strips[g] = strips[g] - column * step
-    out = jnp.concatenate([v * w for v, w in zip(strips, scales)], axis=0)
-    return out[:, n:]
+    count = n // 8
+    strips = [both[8 * g : 8 * g + 8, :] for g in range(count)]
+    for own in range(count):
+        columns = {
+            g: [
+                jnp.broadcast_to(strips[g][:, 8 * own + m : 8 * own + m + 1], full)
+                for m in range(8)
+            ]
+            for g in range(own, count)
+        }
+        lines = [jnp.broadcast_to(strips[own][r : r + 1, :], full) for r in range(8)]
+        corner = {
+            (r, m): jnp.broadcast_to(columns[own][m][r : r + 1, :], full)
+            for r in range(8)
+            for m in range(r, 8)
+        }
+        ratio, inverse, scale = {}, [], []
+        for r in range(8):
+            pivot = corner[r, r]
+            inverse.append(1.0 / pivot)
+            scale.append(lax.rsqrt(pivot))
+            for m in range(r + 1, 8):
+                ratio[r, m] = corner[r, m] * inverse[r]
+            for low in range(r + 1, 8):
+                for m in range(low, 8):
+                    corner[low, m] = corner[low, m] - corner[r, low] * ratio[r, m]
+        for r in range(8):
+            for m in range(r + 1, 8):
+                lines[m] = lines[m] - ratio[r, m] * lines[r]
+        for g in range(own + 1, count):
+            column = columns[g]
+            for r in range(8):
+                for m in range(r + 1, 8):
+                    column[m] = column[m] - column[r] * ratio[r, m]
+            for r in range(8):
+                strips[g] = strips[g] - (column[r] * inverse[r]) * lines[r]
+        done = lines[0] * scale[0]
+        for r in range(1, 8):
+            done = jnp.where(row_id == r, lines[r] * scale[r], done)
+        strips[own] = done
+    return jnp.concatenate(strips, axis=0)[:, n:]
 
 
 def factor_kernel(packed, xg, factor_ref, final_ref, khi, klo, basis, q, work, spread):
@@ -309,12 +343,13 @@
         work[:, pl.ds(0, RANK)] = jnp.zeros((RANK, RANK), jnp.float32)
         work[:, pl.ds(RANK, RANK)] = unit
 
-        @pl.loop(0, 6)
-        def _(i):
-            at = pl.ds(pl.multiple_of(i * BLOCK, BLOCK), BLOCK)
+        for i in range(6):
+            at = pl.ds(i * BLOCK, BLOCK)
             image = nn(khi[at, :], basis[...]) + nn(klo[at, :], basis[...])
             q[at, :] = image
-            work[:, pl.ds(0, RANK)] += tn(basis[at, :].astype(jnp.float32), image, EXACT)
+            parts = split(image)
+            line = basis[at, :].astype(jnp.float32).T.astype(jnp.bfloat16)
+            work[:, pl.ds(0, RANK)] += (nn(line, parts[0]) + nn(line, parts[1])) + nn(line, parts[2])
 
         work[:, pl.ds(0, RANK)] = work[:, pl.ds(0, RANK)] * (1.0 / GRID)
         for p in range(4):

time: 229 us -> 177 us (0.77)
  Pallas kernels: 214 us -> 162 us
    pallas_call x1, Pallas kernels: 110 us -> 57.4 us  [factors(): pl.pallas_call(factor_kernel, out_shape=(jax.ShapeDtypeStruct((SHARD_ROWS...]
where the time goes in v2:
time: 177 us
  Pallas kernels  162 us (92%)
  other arithmetic  8.05 us (5%)
  matrix products  4.25 us (2%)
    pallas_call x1, Pallas kernels, exchange(): pl.pallas_call(exchange_kernel, out_shape=(jax.ShapeDtypeStruct((PACKED,...  105 us
    pallas_call x1, Pallas kernels, factors(): pl.pallas_call(factor_kernel, out_shape=(jax.ShapeDtypeStruct((SHARD_ROWS...  57.4 us
    another operation x6, other arithmetic, refine(): lower_factor = jnp.linalg.cholesky(inner_gram(image_rows) / row_count)  4.28 us
    another operation x4, other arithmetic, solve_right(): lax.linalg.triangular_solve(lower_factor, image_rows, left_side=False, lo...  3.75 us

profile of v2, /device:TPU:1, one launch (start us, length us, event | category | flops | bytes accessed | tf_op | source)
XLA Modules:
  0.0 176.6 jit_solution(6813688774970927299)
XLA Ops:
  0.6 0.0 copy-start
  0.6 0.0 copy-start.1
  0.7 104.5 %moments.1 = (f32[14336,128]{1,0:T(8,128)}, bf16[1536,384]{1,0:T(8,128)(2,1)}) custom-call(bf16[192,1536]{1,0:T(8,128)(2,1)} %x_ref.1, bf16[1536,256]{1,0:T(8,128)(2,1)} %b_ref.1), custom_call_target="tpu_custom_call" | custom-call | tf_op jit(solution)/shard_map/moments/pallas_call | solution.py:226
  105.2 57.4 %passes.1 = (f32[192,256]{1,0:T(8,128)}, bf16[1536,256]{1,0:T(8,128)(2,1)}) custom-call(f32[14336,128]{1,0:T(8,128)} %get-tuple-element.8.packed, bf16[1536,384]{1,0:T(8,128)(2,1)} %get-tuple-element.9.xg), custom_call_target="tpu_custom_call" | custom-call | tf_op jit(solution)/shard_map/passes/pallas_call | solution.py:385
  162.6 1.7 convolution_bitcast_fusion
  164.3 0.0 copy-done
  164.3 0.1 fusion.8
  164.5 0.2 convolution_multiply_fusion.1
  164.6 0.1 copy.8
  164.7 1.5 cholesky.44
  166.2 0.6 compare_reduce_fusion.1
  166.8 0.6 fusion
  167.5 1.2 custom-call.8
  168.7 0.8 fusion.5
  169.5 1.5 reshape.25
  171.0 0.3 fusion.9
  171.4 0.0 copy-done.1
  171.4 0.1 fusion.10
  171.5 0.1 convolution_multiply_fusion
  171.7 0.1 copy.10
  171.7 1.5 cholesky.55
  173.2 0.6 compare_reduce_fusion
  173.9 0.6 fusion.1
  174.5 1.2 custom-call.9
  175.8 0.8 fusion.2
  (4 shorter events, 0.1 us)
Async XLA Ops:
  0.6 163.7 %copy-start = (f32[48,16]{0,1:T(8,128)S(1)}, f32[48,16]{0,1:T(8,128)}, u32[]{:S(2)}) copy-start(f32[48,16]{0,1:T(8,128)} %param.7) | copy-start | bytes 9220
  0.6 170.7 %copy-start.1 = (f32[32,16]{0,1:T(8,128)S(1)}, f32[32,16]{0,1:T(8,128)}, u32[]{:S(2)}) copy-start(f32[32,16]{0,1:T(8,128)} %param.8) | copy-start | bytes 6148

commit v3 on v2

--- a/solution.py
+++ b/solution.py
@@ -17,13 +17,13 @@
 
 BLOCK = 256
 BLOCKS = 7
-PACKED = 28 * 2 * BLOCK
-HALF = PACKED // 2
-RING1 = HALF // 4
-RING2 = RING1 // 4
-LEAF = RING2 // 8
+SPAN = BLOCKS * BLOCK
+HALF = 14 * 2 * BLOCK
 CHIP_COLS = 384
 SHARD_ROWS = 192
+UNITS = (3, 2, 2)
+UNIT = 1024
+COPIES = 200
 
 
 def nt(a, b, precision=None):
@@ -43,7 +43,7 @@
 
 
 def exchange_kernel(
-    x_ref, b_ref, out, xg, acc, aug, r1h, r1f, a2, r2h, r2f, a3, zbuf, send, recv
+    x_ref, b_ref, high, low, xg, out, acc, aug, r1h, r1f, a2, r2h, r2f, a3, zbuf, send, recv
 ):
     s = lax.axis_index("space")
     e = lax.axis_index("ens")
@@ -81,12 +81,10 @@
         pl.semaphore_signal(barrier, inc=1, device_id=d, device_id_type=pl.DeviceIdType.MESH)
     pl.semaphore_wait(barrier, len(greeted))
 
-    used = [0]
     pending = []
 
     def start(src, dst, dev):
-        n = used[0]
-        used[0] += 1
+        n = len(pending)
         copy = pltpu.make_async_remote_copy(
             src_ref=src,
             dst_ref=dst,
@@ -125,96 +123,162 @@
         copy.wait_recv()
     aug[pl.ds(0, ROWS), :] = xg[...]
 
-    @pl.loop(0, 14)
-    def _(k):
-        t = c * 14 + k
+    def block_of(t):
         i = t % BLOCKS
         j = (i + t // BLOCKS) % BLOCKS
-        a = aug[pl.ds(pl.multiple_of(i * BLOCK, BLOCK), BLOCK), :]
-        b = aug[pl.ds(pl.multiple_of(j * BLOCK, BLOCK), BLOCK), :]
-        product = nt(a, b)
-        acc[pl.ds(pl.multiple_of(k * 512, 512), 256), :] = product[:, :128]
-        acc[pl.ds(pl.multiple_of(k * 512 + 256, 256), 256), :] = product[:, 128:]
-
-    def reduce_ring(a, half_in, full_in, place, p, piece, result):
-        to_right, to_left, right, left, opp = place
-        h = piece // 2
-        c1 = start(a.at[rows(opp * piece, h), :], half_in.at[0], to_right)
-        c3 = start(a.at[rows(opp * piece + h, h), :], half_in.at[1], to_left)
-        c2 = start(a.at[rows(right * piece + h, h), :], full_in.at[0, pl.ds(h, h), :], to_right)
-        c4 = start(a.at[rows(left * piece, h), :], full_in.at[1, pl.ds(0, h), :], to_left)
-        c1.wait_recv()
-        a[rows(right * piece, h), :] = a[rows(right * piece, h), :] + half_in[0]
-        c5 = start(a.at[rows(right * piece, h), :], full_in.at[0, pl.ds(0, h), :], to_right)
-        c3.wait_recv()
-        a[rows(left * piece + h, h), :] = a[rows(left * piece + h, h), :] + half_in[1]
-        c6 = start(a.at[rows(left * piece + h, h), :], full_in.at[1, pl.ds(h, h), :], to_left)
-        for copy in (c2, c4, c5, c6):
+        return (
+            pl.ds(pl.multiple_of(i * BLOCK, BLOCK), BLOCK),
+            pl.ds(pl.multiple_of(j * BLOCK, BLOCK), BLOCK),
+        )
+
+    def unpack(core, first, count):
+        @pl.loop(first, first + count)
+        def _(k):
+            at_i, at_j = block_of(core * 14 + k)
+            top = pl.multiple_of(core * HALF + k * 512, 256)
+            block = jnp.concatenate(
+                [out[pl.ds(top, 256), :], out[pl.ds(top + 256, 256), :]], axis=1
+            )
+            for value, r, w in ((block, at_i, at_j), (block.T, at_j, at_i)):
+                first_part = value.astype(jnp.bfloat16)
+                high[r, w] = first_part
+                low[r, w] = (value - first_part.astype(jnp.float32)).astype(jnp.bfloat16)
+
+    def chain(chunk):
+        units = UNITS[chunk]
+        before = sum(UNITS[:chunk])
+        off = before * UNIT
+        clock = 1.9 * before
+
+        @pl.loop(2 * before, 2 * (before + units))
+        def _(k):
+            at_i, at_j = block_of(c * 14 + k)
+            product = nt(aug[at_i, :], aug[at_j, :])
+            acc[pl.ds(pl.multiple_of(k * 512, 512), 256), :] = product[:, :128]
+            acc[pl.ds(pl.multiple_of(k * 512 + 256, 256), 256), :] = product[:, 128:]
+
+        def reduce_ring(a, base, half_in, full_in, place, p, piece, result, at, took):
+            to_right, to_left, right, left, opp = place
+            h = piece // 2
+            hs = pl.ds(at // 2, h)
+
+            def full(side, half):
+                return full_in.at[side, pl.ds(at + half * h, h), :]
+
+            def mine_at(q, half):
+                return rows(base + q * piece + half * h, h)
+
+            c1 = start(a.at[mine_at(opp, 0), :], half_in.at[0, hs, :], to_right)
+            c3 = start(a.at[mine_at(opp, 1), :], half_in.at[1, hs, :], to_left)
+            c2 = start(a.at[mine_at(right, 1), :], full(0, 1), to_right)
+            c4 = start(a.at[mine_at(left, 0), :], full(1, 0), to_left)
+            yield took / 3
+            c1.wait_recv()
+            a[mine_at(right, 0), :] = a[mine_at(right, 0), :] + half_in[0, hs, :]
+            c5 = start(a.at[mine_at(right, 0), :], full(0, 0), to_right)
+            c3.wait_recv()
+            a[mine_at(left, 1), :] = a[mine_at(left, 1), :] + half_in[1, hs, :]
+            c6 = start(a.at[mine_at(left, 1), :], full(1, 1), to_left)
+            yield took
+            for copy in (c2, c4, c5, c6):
+                copy.wait_recv()
+            where = pl.ds(at, piece)
+            result[where, :] = (
+                a[rows(base + p * piece, piece), :] + full_in[0, where, :] + full_in[1, where, :]
+            )
+
+        piece1, piece2, leaf = units * UNIT // 4, units * UNIT // 16, units * UNIT // 128
+        at1, at2, at3 = off // 4, off // 16, off // 128
+        for wait in reduce_ring(acc, off, r1h, r1f, ring1, p1, piece1, a2, at1, 1.9 * units + 2):
+            yield clock + wait
+        clock += 1.9 * units + 2
+        for wait in reduce_ring(a2, at1, r2h, r2f, ring2, p2, piece2, a3, at2, 0.5 * units + 3):
+            yield clock + wait
+        clock += 0.5 * units + 3
+        copies = [
+            start(a3.at[rows(at2 + other * leaf, leaf), :], zbuf.at[k, pl.ds(at3, leaf), :], d)
+            for k, (d, other) in enumerate(zpeers)
+        ]
+        clock += 0.7 * units + 3
+        yield clock
+        total = a3[rows(at2 + z * leaf, leaf), :]
+        for k, copy in enumerate(copies):
             copy.wait_recv()
-        result[...] = a[rows(p * piece, piece), :] + full_in[0] + full_in[1]
-
-    reduce_ring(acc, r1h, r1f, ring1, p1, RING1, a2)
-    reduce_ring(a2, r2h, r2f, ring2, p2, RING2, a3)
-    copies = [
-        start(a3.at[rows(other * LEAF, LEAF), :], zbuf.at[k], d)
-        for k, (d, other) in enumerate(zpeers)
-    ]
-    total = a3[rows(z * LEAF, LEAF), :]
-    for k, copy in enumerate(copies):
-        copy.wait_recv()
-        total = total + zbuf[k]
-
-    base1 = c * HALF
-    base2 = base1 + p1 * RING1
-    base3 = base2 + p2 * RING2
-    leaf = rows(base3 + z * LEAF, LEAF)
-    out[leaf, :] = total
-    copies = [start(out.at[leaf, :], out.at[leaf, :], d) for d, _ in zpeers]
-    for copy in copies:
-        copy.wait_recv()
-
-    def gather_ring(base, place, p, piece, on_piece):
-        to_right, to_left, right, left, _ = place
-        h = piece // 2
-
-        def part(q, half):
-            return rows(base + q * piece + half * h, h)
-
-        def put(q, half, dev):
-            return start(out.at[part(q, half), :], out.at[part(q, half), :], dev)
-
-        r1 = put(p, 0, to_right)
-        l1 = put(p, 1, to_left)
-        r2 = put(p, 1, to_right)
-        l2 = put(p, 0, to_left)
-        on_piece(rows(base + p * piece, piece))
-        r1.wait_recv()
-        r3 = put(left, 0, to_right)
-        on_piece(part(left, 0))
-        l1.wait_recv()
-        l3 = put(right, 1, to_left)
-        on_piece(part(right, 1))
-        r2.wait_recv()
-        on_piece(part(left, 1))
-        l2.wait_recv()
-        on_piece(part(right, 0))
-        r3.wait_recv()
-        opp = (p + 2) % 4
-        on_piece(part(opp, 0))
-        l3.wait_recv()
-        on_piece(part(opp, 1))
-
-    gather_ring(base2, ring2, p2, RING2, lambda where: None)
-    across = []
-    gather_ring(
-        base1,
-        ring1,
-        p1,
-        RING1,
-        lambda where: across.append(start(out.at[where, :], out.at[where, :], partner)),
-    )
-    for copy in across:
-        copy.wait_recv()
+            total = total + zbuf[k, pl.ds(at3, leaf), :]
+
+        base1 = c * HALF + off
+        base2 = base1 + p1 * piece1
+        base3 = base2 + p2 * piece2
+        own = rows(base3 + z * leaf, leaf)
+        out[own, :] = total
+        copies = [start(out.at[own, :], out.at[own, :], d) for d, _ in zpeers]
+        clock += 0.7 * units + 3
+        yield clock
+        for copy in copies:
+            copy.wait_recv()
+
+        def gather_ring(base, place, p, piece, took, on_piece):
+            to_right, to_left, right, left, opp = place
+            h = piece // 2
+
+            def part(q, half):
+                return rows(base + q * piece + half * h, h)
+
+            def put(q, half, dev):
+                return start(out.at[part(q, half), :], out.at[part(q, half), :], dev)
+
+            r1 = put(p, 0, to_right)
+            l1 = put(p, 1, to_left)
+            r2 = put(p, 1, to_right)
+            l2 = put(p, 0, to_left)
+            on_piece(rows(base + p * piece, piece))
+            yield took / 3
+            r1.wait_recv()
+            r3 = put(left, 0, to_right)
+            on_piece(part(left, 0))
+            l1.wait_recv()
+            l3 = put(right, 1, to_left)
+            on_piece(part(right, 1))
+            yield 2 * took / 3
+            r2.wait_recv()
+            on_piece(part(left, 1))
+            l2.wait_recv()
+            on_piece(part(right, 0))
+            yield took
+            r3.wait_recv()
+            on_piece(part(opp, 0))
+            l3.wait_recv()
+            on_piece(part(opp, 1))
+
+        for wait in gather_ring(base2, ring2, p2, piece2, 0.5 * units + 3, lambda where: None):
+            yield clock + wait
+        clock += 0.5 * units + 3
+        across = []
+        for wait in gather_ring(
+            base1,
+            ring1,
+            p1,
+            piece1,
+            1.9 * units + 2,
+            lambda where: across.append(start(out.at[where, :], out.at[where, :], partner)),
+        ):
+            yield clock + wait
+        clock += 1.9 * units + 2
+        unpack(c, 2 * before, 2 * units)
+        yield clock + 3
+        for copy in across:
+            copy.wait_recv()
+        unpack(1 - c, 2 * before, 2 * units)
+
+    chains = {n: chain(n) for n in range(len(UNITS))}
+    due = {n: next(one) for n, one in chains.items()}
+    while due:
+        n = min(due, key=lambda one: due[one])
+        value = next(chains[n], None)
+        if value is None:
+            del due[n]
+        else:
+            due[n] = value
     for copy in pending:
         copy.wait_send()
 
@@ -222,30 +286,31 @@
 def exchange(outlook, basis):
     f32, bf16 = jnp.float32, jnp.bfloat16
     vmem = pl.BlockSpec(memory_space=pltpu.VMEM)
-    copies = 64
     return pl.pallas_call(
         exchange_kernel,
         out_shape=(
-            jax.ShapeDtypeStruct((PACKED, 128), f32),
+            jax.ShapeDtypeStruct((SPAN, SPAN), bf16),
+            jax.ShapeDtypeStruct((SPAN, SPAN), bf16),
             jax.ShapeDtypeStruct((ROWS, CHIP_COLS), bf16),
         ),
         in_specs=[vmem, vmem],
-        out_specs=(vmem, vmem),
+        out_specs=(vmem, vmem, vmem),
         scratch_shapes=[
+            pltpu.VMEM((2 * HALF, 128), f32),
             pltpu.VMEM((HALF, 128), f32),
-            pltpu.VMEM((BLOCKS * BLOCK, CHIP_COLS), bf16),
-            pltpu.VMEM((2, RING1 // 2, 128), f32),
-            pltpu.VMEM((2, RING1, 128), f32),
-            pltpu.VMEM((RING1, 128), f32),
-            pltpu.VMEM((2, RING2 // 2, 128), f32),
-            pltpu.VMEM((2, RING2, 128), f32),
-            pltpu.VMEM((RING2, 128), f32),
-            pltpu.VMEM((7, LEAF, 128), f32),
-            pltpu.SemaphoreType.DMA((copies,)),
-            pltpu.SemaphoreType.DMA((copies,)),
+            pltpu.VMEM((SPAN, CHIP_COLS), bf16),
+            pltpu.VMEM((2, HALF // 8, 128), f32),
+            pltpu.VMEM((2, HALF // 4, 128), f32),
+            pltpu.VMEM((HALF // 4, 128), f32),
+            pltpu.VMEM((2, HALF // 32, 128), f32),
+            pltpu.VMEM((2, HALF // 16, 128), f32),
+            pltpu.VMEM((HALF // 16, 128), f32),
+            pltpu.VMEM((7, HALF // 128, 128), f32),
+            pltpu.SemaphoreType.DMA((COPIES,)),
+            pltpu.SemaphoreType.DMA((COPIES,)),
         ],
         compiler_params=pltpu.CompilerParams(
-            collective_id=0, has_side_effects=True, vmem_limit_bytes=60 << 20
+            collective_id=0, has_side_effects=True, vmem_limit_bytes=36 << 20
         ),
         name="moments",
     )(outlook, basis)
@@ -309,31 +374,9 @@
     return jnp.concatenate(strips, axis=0)[:, n:]
 
 
-def factor_kernel(packed, xg, factor_ref, final_ref, khi, klo, basis, q, work, spread):
+def factor_kernel(high, low, xg, factor_ref, final_ref, basis, q, work, spread):
     core = lax.axis_index("ens") % 2
-    for t in range(28):
-        i = t % BLOCKS
-        j = (i + t // BLOCKS) % BLOCKS
-        if i == j == BLOCKS - 1:
-            continue
-        block = jnp.concatenate(
-            [packed[pl.ds(t * 512, 256), :], packed[pl.ds(t * 512 + 256, 256), :]], axis=1
-        )
-        if i == BLOCKS - 1:
-            basis[pl.ds(j * BLOCK, BLOCK), :] = block.T.astype(jnp.bfloat16)
-            continue
-        hi = block.astype(jnp.bfloat16)
-        if j == BLOCKS - 1:
-            basis[pl.ds(i * BLOCK, BLOCK), :] = hi
-            continue
-        lo = (block - hi.astype(jnp.float32)).astype(jnp.bfloat16)
-        at_i, at_j = pl.ds(i * BLOCK, BLOCK), pl.ds(j * BLOCK, BLOCK)
-        khi[at_i, at_j] = hi
-        klo[at_i, at_j] = lo
-        if i != j:
-            khi[at_j, at_i] = hi.astype(jnp.float32).T.astype(jnp.bfloat16)
-            klo[at_j, at_i] = lo.astype(jnp.float32).T.astype(jnp.bfloat16)
-
+    basis[...] = high[pl.ds(0, ROWS), pl.ds(ROWS, RANK)]
     unit = (
         lax.broadcasted_iota(jnp.int32, (RANK, RANK), 0)
         == lax.broadcasted_iota(jnp.int32, (RANK, RANK), 1)
@@ -345,7 +388,7 @@
 
         for i in range(6):
             at = pl.ds(i * BLOCK, BLOCK)
-            image = nn(khi[at, :], basis[...]) + nn(klo[at, :], basis[...])
+            image = nn(high[at, pl.ds(0, ROWS)], basis[...]) + nn(low[at, pl.ds(0, ROWS)], basis[...])
             q[at, :] = image
             parts = split(image)
             line = basis[at, :].astype(jnp.float32).T.astype(jnp.bfloat16)
@@ -379,7 +422,7 @@
     final_ref[...] = basis[...]
 
 
-def factors(packed, xg):
+def factors(high, low, xg):
     f32, bf16 = jnp.float32, jnp.bfloat16
     vmem = pl.BlockSpec(memory_space=pltpu.VMEM)
     return pl.pallas_call(
@@ -388,19 +431,17 @@
             jax.ShapeDtypeStruct((SHARD_ROWS, RANK), f32),
             jax.ShapeDtypeStruct((ROWS, RANK), bf16),
         ),
-        in_specs=[vmem, vmem],
+        in_specs=[vmem, vmem, vmem],
         out_specs=(vmem, vmem),
         scratch_shapes=[
-            pltpu.VMEM((ROWS, ROWS), bf16),
-            pltpu.VMEM((ROWS, ROWS), bf16),
             pltpu.VMEM((ROWS, RANK), bf16),
             pltpu.VMEM((ROWS, RANK), f32),
             pltpu.VMEM((RANK, 2 * RANK), f32),
             pltpu.VMEM((CHIP_COLS, RANK), f32),
         ],
-        compiler_params=pltpu.CompilerParams(vmem_limit_bytes=60 << 20),
+        compiler_params=pltpu.CompilerParams(vmem_limit_bytes=30 << 20),
         name="passes",
-    )(packed, xg)
+    )(high, low, xg)
 
 
 def inner_gram(image_rows):
@@ -430,8 +471,8 @@
 
 
 def on_device(outlook_array, earlier_location_basis, earlier_ensemble_basis, earlier_height_basis):
-    packed, slab = exchange(outlook_array, earlier_location_basis)
-    factor, final = factors(packed, slab)
+    high, low, slab = exchange(outlook_array, earlier_location_basis)
+    factor, final = factors(high, low, slab)
     member_gram, level_gram = factor_grams(final)
     return (
         factor,

time: 177 us -> 158 us (0.89)
  Pallas kernels: 162 us -> 144 us
    pallas_call x1, Pallas kernels: 105 us -> 91.5 us  [exchange(): pl.pallas_call(exchange_kernel, out_shape=(jax.ShapeDtypeStruct((SPAN, SP...]
    pallas_call x1, Pallas kernels: 57.4 us -> 52.1 us  [factors(): pl.pallas_call(factor_kernel, out_shape=(jax.ShapeDtypeStruct((SHARD_ROWS...]
    unnamed x4 -> x8, local copies, waits for them, and re-layouts: 0.02 us -> 2.23 us
where the time goes in v3:
time: 158 us
  Pallas kernels  144 us (91%)
  other arithmetic  8.05 us (5%)
  matrix products  2.86 us (2%)
  local copies, waits for them, and re-layouts  2.75 us (2%)
    pallas_call x1, Pallas kernels, exchange(): pl.pallas_call(exchange_kernel, out_shape=(jax.ShapeDtypeStruct((SPAN, SP...  91.5 us
    pallas_call x1, Pallas kernels, factors(): pl.pallas_call(factor_kernel, out_shape=(jax.ShapeDtypeStruct((SHARD_ROWS...  52.1 us
    another operation x6, other arithmetic, refine(): lower_factor = jnp.linalg.cholesky(inner_gram(image_rows) / row_count)  4.28 us
    another operation x4, other arithmetic, solve_right(): lax.linalg.triangular_solve(lower_factor, image_rows, left_side=False, lo...  3.75 us

profile of v3, /device:TPU:1, one launch (start us, length us, event | category | flops | bytes accessed | tf_op | source)
XLA Modules:
  0.0 158.0 jit_solution(4442371638593135666)
XLA Ops:
  0.6 0.0 copy-start
  0.6 0.0 copy-start.1
  0.7 1.1 copy-done.1
  1.8 0.0 copy-start.2
  1.8 1.1 copy-done.2
  2.9 91.5 %moments.1 = (bf16[1792,1792]{1,0:T(8,128)(2,1)S(1)}, bf16[1792,1792]{1,0:T(8,128)(2,1)S(1)}, bf16[1536,384]{1,0:T(8,128)(2,1)S(1)}) custom-call(bf16[192,1536]{1,0:T(8,128)(2,1)S(1)} %copy-done.2, bf16[1536,256]{1,0:T(8,128)(2,1)S(1)} %copy-done.1), custom_call_target="tpu_custom_call" | custom-call | tf_op jit(solution)/shard_map/moments/pallas_call | solution.py:289
  94.4 0.0 copy-start.3
  94.4 52.1 %passes.1 = (f32[192,256]{1,0:T(8,128)}, bf16[1536,256]{1,0:T(8,128)(2,1)S(1)}) custom-call(bf16[1792,1792]{1,0:T(8,128)(2,1)S(1)} %get-tuple-element.9.high, bf16[1792,1792]{1,0:T(8,128)(2,1)S(1)} %get-tuple-element.10.low, bf16[1536,384]{1,0:T(8,128)(2,1)S(1)} %get-tuple-element.11.xg), custom_call_target="tpu_custom_call" | custom-call | tf_op jit(solution)/shard_map/passes/pallas_call | solution.py:428
  146.5 0.3 convolution_bitcast_fusion
  146.8 0.0 copy-done
  146.8 0.1 fusion.8
  147.0 0.2 convolution_multiply_fusion.1
  147.1 0.1 copy.8
  147.2 1.5 cholesky.44
  148.7 0.6 compare_reduce_fusion.1
  149.3 0.6 fusion
  150.0 1.2 custom-call.8
  151.2 0.8 fusion.5
  152.0 0.4 reshape.25
  152.4 0.3 fusion.9
  152.7 0.0 copy-done.3
  152.8 0.1 fusion.10
  152.9 0.1 convolution_multiply_fusion
  153.0 0.1 copy.10
  153.1 1.5 cholesky.55
  154.6 0.6 compare_reduce_fusion
  155.3 0.6 fusion.1
  155.9 1.2 custom-call.9
  157.1 0.8 fusion.2
  (4 shorter events, 0.1 us)
Async XLA Ops:
  0.6 146.2 %copy-start = (f32[48,16]{0,1:T(8,128)S(1)}, f32[48,16]{0,1:T(8,128)}, u32[]{:S(2)}) copy-start(f32[48,16]{0,1:T(8,128)} %param.7) | copy-start | bytes 9220
  0.6 1.1 copy-start.1
  1.8 1.1 copy-start.2
  94.4 58.4 %copy-start.3 = (f32[32,16]{0,1:T(8,128)S(1)}, f32[32,16]{0,1:T(8,128)}, u32[]{:S(2)}) copy-start(f32[32,16]{0,1:T(8,128)} %param.8) | copy-start | bytes 6148
